TPU v7x, 32 devices: a whole 2x2x4 slice. The times are simulated.
32 devices in a mesh: pts: 8 (over y, x, core), lst: 4 (over z).
Axes of the slice: x: 2, y: 2, z: 4, core: 2. Of those that a mesh axis runs over, the one named last changes fastest.
Arguments:
- tower_out: bfloat16 [16384, 1024], P('pts', 'lst'), may hold values from -6 to 6
- projection: bfloat16 [1024, 256], P('lst'), may hold values from -1 to 1
- centroids: bfloat16 [16384, 256], P('lst'), may hold values from -6 to 6
Outputs:
- new_centroids: float32 [16384, 256], P(('lst', 'pts'))
- row_log: float32 [16384], P('pts')
All inputs are finite; a program needn't handle non-finite values.
Results may differ from a plain program's by a relative error of at most 0.0045.
Values may be sent and summed in bfloat16 or wider, within the bound.
A program may use at most 64 MiB of HBM per device.

v0:
```python
import jax
import jax.numpy as jnp
from jax import lax
from jax.sharding import PartitionSpec as P

DP = 256
ITERS = 3
temper = 0.05


def rms_norm(values):
    return values * lax.rsqrt(jnp.mean(values * values, axis=-1, keepdims=True) + 1e-06)


def energy(zblock, unit_lists):
    scores = lax.dot_general(
        zblock, unit_lists, (((1,), (1,)), ((), ())), preferred_element_type=jnp.float32
    )
    return jnp.exp(scores / (DP * temper) - 1.0 / temper)


def update_terms(energy_blk, scale_blk, col_scale, zblock):
    weights = (scale_blk[:, None] * energy_blk * col_scale[None, :]).astype(jnp.bfloat16)
    return lax.dot_general(
        weights, zblock, (((0,), (0,)), ((), ())), preferred_element_type=jnp.float32
    )


def column_total(local_sum):
    return lax.psum(local_sum, "pts")


def on_device(tower_out, projection, centroids):
    point_rows = tower_out.shape[0]
    list_count = centroids.shape[0]
    total_points = point_rows * lax.axis_size("pts")
    total_lists = list_count * lax.axis_size("lst")
    balance = total_points / total_lists
    full_rows = lax.all_to_all(tower_out, "lst", split_axis=0, concat_axis=1, tiled=True)
    own_rows = jnp.dot(
        full_rows,
        lax.all_gather(projection, "lst", axis=0, tiled=True),
        preferred_element_type=jnp.float32,
    )
    normed = lax.all_gather(rms_norm(own_rows).astype(jnp.bfloat16), "lst", axis=0, tiled=True)
    unit_lists = rms_norm(centroids.astype(jnp.float32)).astype(jnp.bfloat16)
    block_rows = min(512, point_rows)
    block_count = point_rows // block_rows
    blocks = normed.reshape(block_count, block_rows, DP)
    start_sums = jnp.zeros((list_count, DP), jnp.float32)
    row_scale = jnp.ones((point_rows,), jnp.float32)
    col_scale = jnp.ones((list_count,), jnp.float32)
    for sweep in range(ITERS):

        def column_step(running, inputs):
            zblock, scale_blk = inputs
            return (
                running + jnp.sum(energy(zblock, unit_lists) * scale_blk[:, None], axis=0),
                None,
            )

        column_sum = column_total(
            lax.scan(
                column_step,
                jnp.zeros((list_count,), jnp.float32),
                (blocks, row_scale.reshape(block_count, block_rows)),
            )[0]
        )
        col_scale = balance / column_sum

        def row_step(zblock, scales=col_scale):
            return jnp.sum(energy(zblock, unit_lists) * scales[None, :], axis=1)

        row_local = lax.map(row_step, blocks).reshape(point_rows)
        row_scale = 1.0 / lax.psum(row_local, "lst")

    def update_step(running, inputs):
        zblock, scale_blk = inputs
        return (
            running + update_terms(energy(zblock, unit_lists), scale_blk, col_scale, zblock),
            None,
        )

    list_sums = lax.scan(
        update_step, start_sums, (blocks, row_scale.reshape(block_count, block_rows))
    )[0]
    owned_sums = lax.psum_scatter(list_sums, "pts", scatter_dimension=0, tiled=True)
    return (rms_norm(owned_sums), jnp.log(row_scale))


def solution(mesh):
    return jax.shard_map(
        on_device,
        mesh=mesh,
        in_specs=(P("pts", "lst"), P("lst", None), P("lst", None)),
        out_specs=(P(("lst", "pts"), None), P("pts")),
        check_vma=False,
    )
```

profile of v0, /device:TPU:0, one launch (start us, length us, event | category | flops | bytes accessed | tf_op | source)
XLA Modules:
  0.0 361.7 jit_solution(5650307541410187121)
XLA Ops:
  7.2 0.0 copy-start
  7.2 6.5 %all-to-all-start = ((bf16[4,512,256]{2,1,0:T(8,128)(2,1)}), bf16[4,512,256]{2,1,0:T(8,128)(2,1)S(1)}, u32[]{:S(2)}, u32[]{:S(2)}) async-start(bf16[4,512,256]{2,1,0:T(8,128)(2,1)} %bitcast.90), calls=%async_computation | async-start | bytes 2097152 | tf_op jit(solution)/shard_map/all_to_all | solution.py:39
  13.7 0.0 all-gather.2.cloned.1.call-start
  13.7 36.6 %all_gather.6 = bf16[1024,256]{1,0:T(8,128)(2,1)} all-gather(bf16[256,256]{1,0:T(8,128)(2,1)} %param.18), channel_id=1, replica_groups=mesh['pts'=8,'lst'=4] {'lst'}, dimensions={0}, use_global_device_ids=true | all-gather | bytes 655360 | tf_op jit(solution)/shard_map/all_gather | solution.py:42
  50.2 0.0 all-to-all-done
  50.3 1.3 copy.19
  51.6 1.9 multiply_reduce_fusion.6
  53.5 0.7 multiply_convert_fusion.1
  54.2 0.0 all-gather.2.cloned.1.call-update
  54.2 0.0 reduce-scatter.2.cloned.1.call-start
  54.3 0.0 copy-done
  54.3 0.6 fusion.26
  55.0 1.7 fusion.27
  56.7 26.8 %all-gather.2.cloned.1.call-done = bf16[2048,256]{0,1:T(8,128)(2,1)} async-done(((bf16[512,256]{0,1:T(8,128)(2,1)}), bf16[2048,256]{0,1:T(8,128)(2,1)}) %all-gather.2.cloned.1.call-update) | async-done | bytes 1048592 | tf_op jit(solution)/shard_map/all_gather | solution.py:45
  83.5 1.5 copy.27
  85.0 13.7 %while.91 = (s32[]{:T(128)}, f32[4096]{0:T(1024)S(1)}, bf16[4,512,256]{2,1,0:T(8,128)(2,1)S(1)}, bf16[4096,256]{1,0:T(8,128)(2,1)}, s32[]{:T(128)}, /*index=5*/s32[]{:T(128)}) while((s32[]{:T(128)}, f32[4096]{0:T(1024)S(1)}, bf16[4,512,256]{2,1,0:T(8,128)(2,1)S(1)}, bf16[4096,256]{1,0:T(8,128)(2,1)}, s32[]{:T(128)}, ...), condition=%wide.region_4.5_spmd.clone, body=%wide.region_2.4_spmd.clone.sunk | while | flops 1080037376 | bytes 2424915 | solution.py:63
  85.0 3.4 exponential_reduce_fusion.2
  88.4 3.4 exponential_reduce_fusion.2
  91.9 3.4 exponential_reduce_fusion.2
  95.3 3.4 exponential_reduce_fusion.2
  98.7 23.5 %psum.42 = f32[4096]{0:T(1024)S(1)} all-reduce(f32[4096]{0:T(1024)S(1)} %get-tuple-element.457), channel_id=1, replica_groups=mesh['pts'=8,'lst'=4] {'pts'}, use_global_device_ids=true, to_apply=%region_5.6 | all-reduce | flops 4096 | bytes 32768 | tf_op jit(solution)/shard_map/psum | solution.py:30
  122.2 15.0 %while.88 = (s32[]{:T(128)}, f32[4,512]{1,0:T(4,128)S(1)}, bf16[4,512,256]{2,1,0:T(8,128)(2,1)S(1)}, bf16[4096,256]{1,0:T(8,128)(2,1)}, f32[4096]{0:T(1024)S(1)}, /*index=5*/s32[]{:T(128)}, s32[]{:T(128)}) while((s32[]{:T(128)}, f32[4,512]{1,0:T(4,128)S(1)}, bf16[4,512,256]{2,1,0:T(8,128)(2,1)S(1)}, bf16[4096,256]{1,0:T(8,128)(2,1)}, ...), condition=%wide.region_8.9_spmd, body=%wide.region_6.8_spmd.sunk | while | flops 1082129920 | bytes 2381909 | solution.py:74
  122.3 3.7 %multiply_reduce_fusion.12 = f32[512]{0:T(512)S(1)} fusion(bf16[4096,256]{1,0:T(8,128)(2,1)} %get-tuple-element.967, f32[4096]{0:T(1024)S(1)} %get-tuple-element.968, bf16[4,512,256]{2,1,0:T(8,128)(2,1)S(1)} %get-tuple-element.966, s32[]{:T(128)} %get-tuple-element.957), kind=kOutput, calls=%fused_computation.clone.1 | convolution fusion | flops 1082129920 | bytes 2377732 | tf_op jit(solution)/shard_map/while/body/eval_jaxpr/dot_general | solution.py:16
  126.0 3.7 %multiply_reduce_fusion.12 = f32[512]{0:T(512)S(1)} fusion(bf16[4096,256]{1,0:T(8,128)(2,1)} %get-tuple-element.967, f32[4096]{0:T(1024)S(1)} %get-tuple-element.968, bf16[4,512,256]{2,1,0:T(8,128)(2,1)S(1)} %get-tuple-element.966, s32[]{:T(128)} %get-tuple-element.957), kind=kOutput, calls=%fused_computation.clone.1 | convolution fusion | flops 1082129920 | bytes 2377732 | tf_op jit(solution)/shard_map/while/body/eval_jaxpr/dot_general | solution.py:16
  129.8 3.7 %multiply_reduce_fusion.12 = f32[512]{0:T(512)S(1)} fusion(bf16[4096,256]{1,0:T(8,128)(2,1)} %get-tuple-element.967, f32[4096]{0:T(1024)S(1)} %get-tuple-element.968, bf16[4,512,256]{2,1,0:T(8,128)(2,1)S(1)} %get-tuple-element.966, s32[]{:T(128)} %get-tuple-element.957), kind=kOutput, calls=%fused_computation.clone.1 | convolution fusion | flops 1082129920 | bytes 2377732 | tf_op jit(solution)/shard_map/while/body/eval_jaxpr/dot_general | solution.py:16
  133.5 3.7 %multiply_reduce_fusion.12 = f32[512]{0:T(512)S(1)} fusion(bf16[4096,256]{1,0:T(8,128)(2,1)} %get-tuple-element.967, f32[4096]{0:T(1024)S(1)} %get-tuple-element.968, bf16[4,512,256]{2,1,0:T(8,128)(2,1)S(1)} %get-tuple-element.966, s32[]{:T(128)} %get-tuple-element.957), kind=kOutput, calls=%fused_computation.clone.1 | convolution fusion | flops 1082129920 | bytes 2377732 | tf_op jit(solution)/shard_map/while/body/eval_jaxpr/dot_general | solution.py:16
  137.3 10.9 %psum.43 = f32[2048]{0:T(1024)S(1)} all-reduce(f32[2048]{0:T(1024)S(1)} %bitcast.102), channel_id=1, replica_groups=mesh['pts'=8,'lst'=4] {'lst'}, use_global_device_ids=true, to_apply=%region_9.10 | all-reduce | flops 2048 | bytes 16384 | tf_op jit(solution)/shard_map/psum | solution.py:75
  148.2 14.9 %while.92 = (s32[]{:T(128)}, f32[4096]{0:T(1024)S(1)}, bf16[4,512,256]{2,1,0:T(8,128)(2,1)S(1)}, bf16[4096,256]{1,0:T(8,128)(2,1)}, f32[4,512]{1,0:T(4,128)S(1)}, /*index=5*/s32[]{:T(128)}, s32[]{:T(128)}) while((s32[]{:T(128)}, f32[4096]{0:T(1024)S(1)}, bf16[4,512,256]{2,1,0:T(8,128)(2,1)S(1)}, bf16[4096,256]{1,0:T(8,128)(2,1)}, ...), condition=%wide.region_12.13_spmd.clone, body=%wide.region_10.12_spmd.clone.sunk | while | flops 1082134528 | bytes 2431071 | solution.py:63
  148.2 3.7 %multiply_reduce_fusion.15 = f32[4096]{0:T(1024)S(1)} fusion(bf16[4096,256]{1,0:T(8,128)(2,1)} %get-tuple-element.988, f32[512]{0:T(512)S(1)} %bitcast.97, bf16[4,512,256]{2,1,0:T(8,128)(2,1)S(1)} %get-tuple-element.987, s32[]{:T(128)} %get-tuple-element.978), kind=kOutput, calls=%fused_computation.17.clone.1 | convolution fusion | flops 1082126336 | bytes 2377732 | tf_op jit(solution)/shard_map/while/body/eval_jaxpr/dot_general | solution.py:16
  151.9 3.7 %multiply_reduce_fusion.15 = f32[4096]{0:T(1024)S(1)} fusion(bf16[4096,256]{1,0:T(8,128)(2,1)} %get-tuple-element.988, f32[512]{0:T(512)S(1)} %bitcast.97, bf16[4,512,256]{2,1,0:T(8,128)(2,1)S(1)} %get-tuple-element.987, s32[]{:T(128)} %get-tuple-element.978), kind=kOutput, calls=%fused_computation.17.clone.1 | convolution fusion | flops 1082126336 | bytes 2377732 | tf_op jit(solution)/shard_map/while/body/eval_jaxpr/dot_general | solution.py:16
  155.7 3.7 %multiply_reduce_fusion.15 = f32[4096]{0:T(1024)S(1)} fusion(bf16[4096,256]{1,0:T(8,128)(2,1)} %get-tuple-element.988, f32[512]{0:T(512)S(1)} %bitcast.97, bf16[4,512,256]{2,1,0:T(8,128)(2,1)S(1)} %get-tuple-element.987, s32[]{:T(128)} %get-tuple-element.978), kind=kOutput, calls=%fused_computation.17.clone.1 | convolution fusion | flops 1082126336 | bytes 2377732 | tf_op jit(solution)/shard_map/while/body/eval_jaxpr/dot_general | solution.py:16
  159.4 3.7 %multiply_reduce_fusion.15 = f32[4096]{0:T(1024)S(1)} fusion(bf16[4096,256]{1,0:T(8,128)(2,1)} %get-tuple-element.988, f32[512]{0:T(512)S(1)} %bitcast.97, bf16[4,512,256]{2,1,0:T(8,128)(2,1)S(1)} %get-tuple-element.987, s32[]{:T(128)} %get-tuple-element.978), kind=kOutput, calls=%fused_computation.17.clone.1 | convolution fusion | flops 1082126336 | bytes 2377732 | tf_op jit(solution)/shard_map/while/body/eval_jaxpr/dot_general | solution.py:16
  163.1 22.3 %psum.44 = f32[4096]{0:T(1024)S(1)} all-reduce(f32[4096]{0:T(1024)S(1)} %get-tuple-element.459), channel_id=1, replica_groups=mesh['pts'=8,'lst'=4] {'pts'}, use_global_device_ids=true, to_apply=%region_13.14 | all-reduce | flops 4096 | bytes 32768 | tf_op jit(solution)/shard_map/psum | solution.py:30
  185.4 15.0 %while.89 = (s32[]{:T(128)}, f32[4,512]{1,0:T(4,128)S(1)}, bf16[4,512,256]{2,1,0:T(8,128)(2,1)S(1)}, bf16[4096,256]{1,0:T(8,128)(2,1)}, f32[4096]{0:T(1024)S(1)}, /*index=5*/s32[]{:T(128)}, s32[]{:T(128)}) while((s32[]{:T(128)}, f32[4,512]{1,0:T(4,128)S(1)}, bf16[4,512,256]{2,1,0:T(8,128)(2,1)S(1)}, bf16[4096,256]{1,0:T(8,128)(2,1)}, ...), condition=%wide.region_16.17_spmd, body=%wide.region_14.16_spmd.sunk | while | flops 1082129920 | bytes 2381909 | solution.py:74
  185.4 3.7 %multiply_reduce_fusion.13 = f32[512]{0:T(512)S(1)} fusion(bf16[4096,256]{1,0:T(8,128)(2,1)} %get-tuple-element.1009, f32[4096]{0:T(1024)S(1)} %get-tuple-element.1010, bf16[4,512,256]{2,1,0:T(8,128)(2,1)S(1)} %get-tuple-element.1008, s32[]{:T(128)} %get-tuple-element.999), kind=kOutput, calls=%fused_computation.4.clone.1 | convolution fusion | flops 1082129920 | bytes 2377732 | tf_op jit(solution)/shard_map/while/body/eval_jaxpr/dot_general | solution.py:16
  189.2 3.7 %multiply_reduce_fusion.13 = f32[512]{0:T(512)S(1)} fusion(bf16[4096,256]{1,0:T(8,128)(2,1)} %get-tuple-element.1009, f32[4096]{0:T(1024)S(1)} %get-tuple-element.1010, bf16[4,512,256]{2,1,0:T(8,128)(2,1)S(1)} %get-tuple-element.1008, s32[]{:T(128)} %get-tuple-element.999), kind=kOutput, calls=%fused_computation.4.clone.1 | convolution fusion | flops 1082129920 | bytes 2377732 | tf_op jit(solution)/shard_map/while/body/eval_jaxpr/dot_general | solution.py:16
  192.9 3.7 %multiply_reduce_fusion.13 = f32[512]{0:T(512)S(1)} fusion(bf16[4096,256]{1,0:T(8,128)(2,1)} %get-tuple-element.1009, f32[4096]{0:T(1024)S(1)} %get-tuple-element.1010, bf16[4,512,256]{2,1,0:T(8,128)(2,1)S(1)} %get-tuple-element.1008, s32[]{:T(128)} %get-tuple-element.999), kind=kOutput, calls=%fused_computation.4.clone.1 | convolution fusion | flops 1082129920 | bytes 2377732 | tf_op jit(solution)/shard_map/while/body/eval_jaxpr/dot_general | solution.py:16
  196.7 3.7 %multiply_reduce_fusion.13 = f32[512]{0:T(512)S(1)} fusion(bf16[4096,256]{1,0:T(8,128)(2,1)} %get-tuple-element.1009, f32[4096]{0:T(1024)S(1)} %get-tuple-element.1010, bf16[4,512,256]{2,1,0:T(8,128)(2,1)S(1)} %get-tuple-element.1008, s32[]{:T(128)} %get-tuple-element.999), kind=kOutput, calls=%fused_computation.4.clone.1 | convolution fusion | flops 1082129920 | bytes 2377732 | tf_op jit(solution)/shard_map/while/body/eval_jaxpr/dot_general | solution.py:16
  200.4 8.7 %psum.45 = f32[2048]{0:T(1024)S(1)} all-reduce(f32[2048]{0:T(1024)S(1)} %bitcast.103), channel_id=1, replica_groups=mesh['pts'=8,'lst'=4] {'lst'}, use_global_device_ids=true, to_apply=%region_17.18 | all-reduce | flops 2048 | bytes 16384 | tf_op jit(solution)/shard_map/psum | solution.py:75
  209.2 14.9 %while.93 = (s32[]{:T(128)}, f32[4096]{0:T(1024)S(1)}, bf16[4,512,256]{2,1,0:T(8,128)(2,1)S(1)}, bf16[4096,256]{1,0:T(8,128)(2,1)}, f32[4,512]{1,0:T(4,128)S(1)}, /*index=5*/s32[]{:T(128)}, s32[]{:T(128)}) while((s32[]{:T(128)}, f32[4096]{0:T(1024)S(1)}, bf16[4,512,256]{2,1,0:T(8,128)(2,1)S(1)}, bf16[4096,256]{1,0:T(8,128)(2,1)}, ...), condition=%wide.region_20.21_spmd.clone, body=%wide.region_18.20_spmd.clone.sunk | while | flops 1082134528 | bytes 2431071 | solution.py:63
  209.2 3.7 %multiply_reduce_fusion.16 = f32[4096]{0:T(1024)S(1)} fusion(bf16[4096,256]{1,0:T(8,128)(2,1)} %get-tuple-element.1030, f32[512]{0:T(512)S(1)} %bitcast.98, bf16[4,512,256]{2,1,0:T(8,128)(2,1)S(1)} %get-tuple-element.1029, s32[]{:T(128)} %get-tuple-element.1020), kind=kOutput, calls=%fused_computation.23.clone.1 | convolution fusion | flops 1082126336 | bytes 2377732 | tf_op jit(solution)/shard_map/while/body/eval_jaxpr/dot_general | solution.py:16
  212.9 3.7 %multiply_reduce_fusion.16 = f32[4096]{0:T(1024)S(1)} fusion(bf16[4096,256]{1,0:T(8,128)(2,1)} %get-tuple-element.1030, f32[512]{0:T(512)S(1)} %bitcast.98, bf16[4,512,256]{2,1,0:T(8,128)(2,1)S(1)} %get-tuple-element.1029, s32[]{:T(128)} %get-tuple-element.1020), kind=kOutput, calls=%fused_computation.23.clone.1 | convolution fusion | flops 1082126336 | bytes 2377732 | tf_op jit(solution)/shard_map/while/body/eval_jaxpr/dot_general | solution.py:16
  216.6 3.7 %multiply_reduce_fusion.16 = f32[4096]{0:T(1024)S(1)} fusion(bf16[4096,256]{1,0:T(8,128)(2,1)} %get-tuple-element.1030, f32[512]{0:T(512)S(1)} %bitcast.98, bf16[4,512,256]{2,1,0:T(8,128)(2,1)S(1)} %get-tuple-element.1029, s32[]{:T(128)} %get-tuple-element.1020), kind=kOutput, calls=%fused_computation.23.clone.1 | convolution fusion | flops 1082126336 | bytes 2377732 | tf_op jit(solution)/shard_map/while/body/eval_jaxpr/dot_general | solution.py:16
  220.4 3.7 %multiply_reduce_fusion.16 = f32[4096]{0:T(1024)S(1)} fusion(bf16[4096,256]{1,0:T(8,128)(2,1)} %get-tuple-element.1030, f32[512]{0:T(512)S(1)} %bitcast.98, bf16[4,512,256]{2,1,0:T(8,128)(2,1)S(1)} %get-tuple-element.1029, s32[]{:T(128)} %get-tuple-element.1020), kind=kOutput, calls=%fused_computation.23.clone.1 | convolution fusion | flops 1082126336 | bytes 2377732 | tf_op jit(solution)/shard_map/while/body/eval_jaxpr/dot_general | solution.py:16
  224.0 22.3 %psum.46 = f32[4096]{0:T(1024)S(1)} all-reduce(f32[4096]{0:T(1024)S(1)} %get-tuple-element.461), channel_id=1, replica_groups=mesh['pts'=8,'lst'=4] {'pts'}, use_global_device_ids=true, to_apply=%region_21.22 | all-reduce | flops 4096 | bytes 32768 | tf_op jit(solution)/shard_map/psum | solution.py:30
  246.4 15.1 %while.90 = (s32[]{:T(128)}, f32[4,512]{1,0:T(4,128)S(1)}, bf16[4,512,256]{2,1,0:T(8,128)(2,1)S(1)}, bf16[4096,256]{1,0:T(8,128)(2,1)}, f32[4096]{0:T(1024)S(1)}, /*index=5*/s32[]{:T(128)}, s32[]{:T(128)}) while((s32[]{:T(128)}, f32[4,512]{1,0:T(4,128)S(1)}, bf16[4,512,256]{2,1,0:T(8,128)(2,1)S(1)}, bf16[4096,256]{1,0:T(8,128)(2,1)}, ...), condition=%wide.region_24.25_spmd, body=%wide.region_22.24_spmd.sunk | while | flops 1082129920 | bytes 2381909 | solution.py:74
  246.4 3.7 %multiply_reduce_fusion.14 = f32[512]{0:T(512)S(1)} fusion(bf16[4096,256]{1,0:T(8,128)(2,1)} %get-tuple-element.1051, f32[4096]{0:T(1024)S(1)} %get-tuple-element.1052, bf16[4,512,256]{2,1,0:T(8,128)(2,1)S(1)} %get-tuple-element.1050, s32[]{:T(128)} %get-tuple-element.1041), kind=kOutput, calls=%fused_computation.8.clone.1 | convolution fusion | flops 1082129920 | bytes 2377732 | tf_op jit(solution)/shard_map/while/body/eval_jaxpr/dot_general | solution.py:16
  250.2 3.7 %multiply_reduce_fusion.14 = f32[512]{0:T(512)S(1)} fusion(bf16[4096,256]{1,0:T(8,128)(2,1)} %get-tuple-element.1051, f32[4096]{0:T(1024)S(1)} %get-tuple-element.1052, bf16[4,512,256]{2,1,0:T(8,128)(2,1)S(1)} %get-tuple-element.1050, s32[]{:T(128)} %get-tuple-element.1041), kind=kOutput, calls=%fused_computation.8.clone.1 | convolution fusion | flops 1082129920 | bytes 2377732 | tf_op jit(solution)/shard_map/while/body/eval_jaxpr/dot_general | solution.py:16
  253.9 3.7 %multiply_reduce_fusion.14 = f32[512]{0:T(512)S(1)} fusion(bf16[4096,256]{1,0:T(8,128)(2,1)} %get-tuple-element.1051, f32[4096]{0:T(1024)S(1)} %get-tuple-element.1052, bf16[4,512,256]{2,1,0:T(8,128)(2,1)S(1)} %get-tuple-element.1050, s32[]{:T(128)} %get-tuple-element.1041), kind=kOutput, calls=%fused_computation.8.clone.1 | convolution fusion | flops 1082129920 | bytes 2377732 | tf_op jit(solution)/shard_map/while/body/eval_jaxpr/dot_general | solution.py:16
  257.7 3.7 %multiply_reduce_fusion.14 = f32[512]{0:T(512)S(1)} fusion(bf16[4096,256]{1,0:T(8,128)(2,1)} %get-tuple-element.1051, f32[4096]{0:T(1024)S(1)} %get-tuple-element.1052, bf16[4,512,256]{2,1,0:T(8,128)(2,1)S(1)} %get-tuple-element.1050, s32[]{:T(128)} %get-tuple-element.1041), kind=kOutput, calls=%fused_computation.8.clone.1 | convolution fusion | flops 1082129920 | bytes 2377732 | tf_op jit(solution)/shard_map/while/body/eval_jaxpr/dot_general | solution.py:16
  261.5 10.5 %psum.47 = f32[2048]{0:T(1024)S(1)} all-reduce(f32[2048]{0:T(1024)S(1)} %bitcast.104), channel_id=1, replica_groups=mesh['pts'=8,'lst'=4] {'lst'}, use_global_device_ids=true, to_apply=%region_25.26 | all-reduce | flops 2048 | bytes 16384 | tf_op jit(solution)/shard_map/psum | solution.py:75
  272.0 0.6 fusion.28
  272.7 31.3 %while.94 = (s32[]{:T(128)}, f32[4096,256]{1,0:T(8,128)}, f32[4,512]{1,0:T(4,128)S(1)}, bf16[4,512,256]{2,1,0:T(8,128)(2,1)S(1)}, bf16[4096,256]{1,0:T(8,128)(2,1)}, /*index=5*/f32[4096]{0:T(1024)S(1)}, s32[]{:T(128)}, s32[]{:T(128)}) while((s32[]{:T(128)}, f32[4096,256]{1,0:T(8,128)}, f32[4,512]{1,0:T(4,128)S(1)}, ...), condition=%wide.region_27.28_spmd.clone, body=%wide.region_26.27_spmd.clone.sunk | while | flops 2160066560 | bytes 11033699 | solution.py:84
  272.7 6.9 %convolution_add_fusion.2 = f32[4096,256]{1,0:T(8,128)} fusion(f32[4096,256]{1,0:T(8,128)} %get-tuple-element.1064, pred[]{:T(512)S(6)} %compare.15, bf16[4096,256]{1,0:T(8,128)(2,1)} %get-tuple-element.1075, f32[4096]{0:T(1024)S(1)} %get-tuple-element.1076, f32[512]{0:T(512)S(1)} %bitcast.93, bf16[4,512,256]{2,1,0:T(8,128)(2,1)S(1)} %get-tuple-element.1074, ...), kind=kOutput, calls=%fused_computation.30.clone.1 | convolution fusion | flops 2160066560 | bytes 11029505 | tf_op jit(solution)/shard_map/while/body/eval_jaxpr/dot_general | solution.py:24
  279.6 8.1 %convolution_add_fusion.2 = f32[4096,256]{1,0:T(8,128)} fusion(f32[4096,256]{1,0:T(8,128)} %get-tuple-element.1064, pred[]{:T(512)S(6)} %compare.15, bf16[4096,256]{1,0:T(8,128)(2,1)} %get-tuple-element.1075, f32[4096]{0:T(1024)S(1)} %get-tuple-element.1076, f32[512]{0:T(512)S(1)} %bitcast.93, bf16[4,512,256]{2,1,0:T(8,128)(2,1)S(1)} %get-tuple-element.1074, ...), kind=kOutput, calls=%fused_computation.30.clone.1 | convolution fusion | flops 2160066560 | bytes 11029505 | tf_op jit(solution)/shard_map/while/body/eval_jaxpr/dot_general | solution.py:24
  287.7 8.1 %convolution_add_fusion.2 = f32[4096,256]{1,0:T(8,128)} fusion(f32[4096,256]{1,0:T(8,128)} %get-tuple-element.1064, pred[]{:T(512)S(6)} %compare.15, bf16[4096,256]{1,0:T(8,128)(2,1)} %get-tuple-element.1075, f32[4096]{0:T(1024)S(1)} %get-tuple-element.1076, f32[512]{0:T(512)S(1)} %bitcast.93, bf16[4,512,256]{2,1,0:T(8,128)(2,1)S(1)} %get-tuple-element.1074, ...), kind=kOutput, calls=%fused_computation.30.clone.1 | convolution fusion | flops 2160066560 | bytes 11029505 | tf_op jit(solution)/shard_map/while/body/eval_jaxpr/dot_general | solution.py:24
  295.8 8.1 %convolution_add_fusion.2 = f32[4096,256]{1,0:T(8,128)} fusion(f32[4096,256]{1,0:T(8,128)} %get-tuple-element.1064, pred[]{:T(512)S(6)} %compare.15, bf16[4096,256]{1,0:T(8,128)(2,1)} %get-tuple-element.1075, f32[4096]{0:T(1024)S(1)} %get-tuple-element.1076, f32[512]{0:T(512)S(1)} %bitcast.93, bf16[4,512,256]{2,1,0:T(8,128)(2,1)S(1)} %get-tuple-element.1074, ...), kind=kOutput, calls=%fused_computation.30.clone.1 | convolution fusion | flops 2160066560 | bytes 11029505 | tf_op jit(solution)/shard_map/while/body/eval_jaxpr/dot_general | solution.py:24
  304.0 0.0 reduce-scatter.2.cloned.1.call-update
  304.0 47.7 %reduce-scatter.2.cloned.1.call-done = f32[512,256]{1,0:T(8,128)} async-done(((f32[4096,256]{1,0:T(8,128)}), f32[512,256]{1,0:T(8,128)}) %reduce-scatter.2.cloned.1.call-update) | async-done | bytes 524304 | tf_op jit(solution)/shard_map/reduce_scatter | solution.py:87
  351.7 1.2 multiply_reduce_fusion.5
  352.9 2.0 broadcast_multiply_fusion
  (57 shorter events, 0.8 us)
Async XLA Ops:
  7.2 47.2 %copy-start = (bf16[4096,256]{1,0:T(8,128)(2,1)S(1)}, bf16[4096,256]{1,0:T(8,128)(2,1)}, u32[]{:S(2)}) copy-start(bf16[4096,256]{1,0:T(8,128)(2,1)} %param.19) | copy-start | bytes 6291460
  7.2 43.1 %all-to-all-start = ((bf16[4,512,256]{2,1,0:T(8,128)(2,1)}), bf16[4,512,256]{2,1,0:T(8,128)(2,1)S(1)}, u32[]{:S(2)}, u32[]{:S(2)}) async-start(bf16[4,512,256]{2,1,0:T(8,128)(2,1)} %bitcast.90), calls=%async_computation | async-start | bytes 2097152 | tf_op jit(solution)/shard_map/all_to_all | solution.py:39
  13.7 69.8 %all-gather.2.cloned.1.call-start = ((), (), s32[]{:S(2)}) async-start(), calls=%async_computation.2 | async-start | bytes 1310720 | tf_op jit(solution)/shard_map/all_gather | solution.py:45
  54.2 297.4 %reduce-scatter.2.cloned.1.call-start = ((), (), s32[]{:S(2)}) async-start(), calls=%async_computation.3 | async-start | bytes 4718592 | tf_op jit(solution)/shard_map/reduce_scatter | solution.py:87
Sparse Core Ops, SparseCore 0:
  54.3 29.1 all-gather.1
  304.1 47.5 reduce-scatter.1
where the time goes:
time: 363 us; the launch traced here: 362 us
  blocking collectives  135 us (37%)
  matrix products  120 us (33%)
  waiting for transfers between devices  74.5 us (21%)
  between operations  14.2 us (4%)
  other arithmetic  7 us (2%)
  starting transfers between devices  6.53 us (2%)
    dot_general x24, matrix products, energy(): lax.dot_general(zblock, unit_lists, (((1,), (1,)), ((), ())), preferred_e...  87.2 us
    psum x3, blocking collectives, column_total(): return lax.psum(local_sum, 'pts')  68.1 us
    reduce_scatter x1, waiting for transfers between devices, on_device(): lax.psum_scatter(list_sums, 'pts', scatter_dimension=0, tiled=True)  47.7 us
    all_gather x1, blocking collectives, on_device(): lax.all_gather(projection, 'lst', axis=0, tiled=True)  36.6 us
    dot_general x4, matrix products, update_terms(): lax.dot_general(weights, zblock, (((0,), (0,)), ((), ())), preferred_elem...  31.2 us
    psum x3, blocking collectives, on_device(): row_scale = 1.0 / lax.psum(row_local, 'lst')  30.1 us
    all_gather x1, waiting for transfers between devices, on_device(): lax.all_gather(rms_norm(own_rows).astype(jnp.bfloat16), 'lst', axis=0, ti...  26.8 us
  transfers between devices with their start and end apart: 3, of which 2 were waited for; matrix products, arithmetic and copies ran while one was open for 1% of the time, Pallas kernels for 0%

commit v1 on v0

--- a/solution.py
+++ b/solution.py
@@ -6,6 +6,9 @@
 DP = 256
 ITERS = 3
 temper = 0.05
+expand_the_joints = lambda array_here, mesh_ax: jnp.sum(
+    jax.lax.all_gather(array_here, axis_name=mesh_ax), 0
+)
 
 
 def rms_norm(values):
@@ -27,7 +30,7 @@
 
 
 def column_total(local_sum):
-    return lax.psum(local_sum, "pts")
+    return expand_the_joints(local_sum, "pts")
 
 
 def on_device(tower_out, projection, centroids):

time: 363 us -> 322 us (0.89)
  blocking collectives: 135 us -> 92.7 us
    psum x3 -> x0, blocking collectives: 68.1 us -> none  [column_total(): return lax.psum(local_sum, 'pts')]
    all_gather x0 -> x3, blocking collectives: none -> 26.6 us  [jax.lax.all_gather(array_here, axis_name=mesh_ax)]
where the time goes in v1:
time: 322 us; the launch traced here: 321 us
  matrix products  120 us (37%)
  blocking collectives  92.7 us (29%)
  waiting for transfers between devices  75.4 us (23%)
  between operations  14.3 us (4%)
  other arithmetic  7.1 us (2%)
  starting transfers between devices  6.53 us (2%)
  local copies, waits for them, and re-layouts  3.6 us (1%)
    dot_general x24, matrix products, energy(): lax.dot_general(zblock, unit_lists, (((1,), (1,)), ((), ())), preferred_e...  87.2 us
    reduce_scatter x1, waiting for transfers between devices, on_device(): lax.psum_scatter(list_sums, 'pts', scatter_dimension=0, tiled=True)  48.6 us
    all_gather x1, blocking collectives, on_device(): lax.all_gather(projection, 'lst', axis=0, tiled=True)  36.6 us
    dot_general x4, matrix products, update_terms(): lax.dot_general(weights, zblock, (((0,), (0,)), ((), ())), preferred_elem...  31.3 us
    psum x3, blocking collectives, on_device(): row_scale = 1.0 / lax.psum(row_local, 'lst')  29.5 us
    all_gather x1, waiting for transfers between devices, on_device(): lax.all_gather(rms_norm(own_rows).astype(jnp.bfloat16), 'lst', axis=0, ti...  26.8 us
    all_gather x3, blocking collectives, jax.lax.all_gather(array_here, axis_name=mesh_ax)  26.6 us
    all_to_all x1, starting transfers between devices, on_device(): lax.all_to_all(tower_out, 'lst', split_axis=0, concat_axis=1, tiled=True)  6.49 us
  transfers between devices with their start and end apart: 3, of which 2 were waited for; matrix products, arithmetic and copies ran while one was open for 1% of the time, Pallas kernels for 0%

profile of v1, /device:TPU:0, one launch (start us, length us, event | category | flops | bytes accessed | tf_op | source)
XLA Modules:
  0.0 320.7 jit_solution(9580894805204322856)
XLA Ops:
  7.2 0.0 copy-start
  7.2 6.5 %all-to-all-start = ((bf16[4,512,256]{2,1,0:T(8,128)(2,1)}), bf16[4,512,256]{2,1,0:T(8,128)(2,1)S(1)}, u32[]{:S(2)}, u32[]{:S(2)}) async-start(bf16[4,512,256]{2,1,0:T(8,128)(2,1)} %bitcast.90), calls=%async_computation | async-start | bytes 2097152 | tf_op jit(solution)/shard_map/all_to_all | solution.py:42
  13.7 0.0 all-gather.5.cloned.1.call-start
  13.7 36.6 %all_gather.24 = bf16[1024,256]{1,0:T(8,128)(2,1)} all-gather(bf16[256,256]{1,0:T(8,128)(2,1)} %param.18), channel_id=1, replica_groups=mesh['pts'=8,'lst'=4] {'lst'}, dimensions={0}, use_global_device_ids=true | all-gather | bytes 655360 | tf_op jit(solution)/shard_map/all_gather | solution.py:45
  50.2 0.0 all-to-all-done
  50.3 1.3 copy.35
  51.6 1.9 multiply_reduce_fusion.6
  53.5 0.7 multiply_convert_fusion.1
  54.2 0.0 all-gather.5.cloned.1.call-update
  54.2 0.0 reduce-scatter.2.cloned.1.call-start
  54.3 0.0 copy-done
  54.3 0.6 fusion.26
  55.0 1.7 fusion.27
  56.7 26.8 %all-gather.5.cloned.1.call-done = bf16[2048,256]{0,1:T(8,128)(2,1)} async-done(((bf16[512,256]{0,1:T(8,128)(2,1)}), bf16[2048,256]{0,1:T(8,128)(2,1)}) %all-gather.5.cloned.1.call-update) | async-done | bytes 1048592 | tf_op jit(solution)/shard_map/all_gather | solution.py:48
  83.5 1.5 copy.43
  85.0 13.7 %while.91 = (s32[]{:T(128)}, f32[4096]{0:T(1024)S(1)}, bf16[4,512,256]{2,1,0:T(8,128)(2,1)S(1)}, bf16[4096,256]{1,0:T(8,128)(2,1)}, s32[]{:T(128)}, /*index=5*/s32[]{:T(128)}) while((s32[]{:T(128)}, f32[4096]{0:T(1024)S(1)}, bf16[4,512,256]{2,1,0:T(8,128)(2,1)S(1)}, bf16[4096,256]{1,0:T(8,128)(2,1)}, s32[]{:T(128)}, ...), condition=%wide.region_4.5_spmd.clone, body=%wide.region_2.4_spmd.clone.sunk | while | flops 1080037376 | bytes 2424915 | solution.py:66
  85.0 3.4 %exponential_reduce_fusion.2 = f32[4096]{0:T(1024)S(1)} fusion(bf16[4096,256]{1,0:T(8,128)(2,1)} %get-tuple-element.1017, bf16[4,512,256]{2,1,0:T(8,128)(2,1)S(1)} %get-tuple-element.1016, s32[]{:T(128)} %get-tuple-element.1008), kind=kOutput, calls=%fused_computation.12.clone.1 | convolution fusion | flops 1080029184 | bytes 2375684 | tf_op jit(solution)/shard_map/while/body/eval_jaxpr/dot_general | solution.py:19
  88.4 3.4 %exponential_reduce_fusion.2 = f32[4096]{0:T(1024)S(1)} fusion(bf16[4096,256]{1,0:T(8,128)(2,1)} %get-tuple-element.1017, bf16[4,512,256]{2,1,0:T(8,128)(2,1)S(1)} %get-tuple-element.1016, s32[]{:T(128)} %get-tuple-element.1008), kind=kOutput, calls=%fused_computation.12.clone.1 | convolution fusion | flops 1080029184 | bytes 2375684 | tf_op jit(solution)/shard_map/while/body/eval_jaxpr/dot_general | solution.py:19
  91.9 3.4 %exponential_reduce_fusion.2 = f32[4096]{0:T(1024)S(1)} fusion(bf16[4096,256]{1,0:T(8,128)(2,1)} %get-tuple-element.1017, bf16[4,512,256]{2,1,0:T(8,128)(2,1)S(1)} %get-tuple-element.1016, s32[]{:T(128)} %get-tuple-element.1008), kind=kOutput, calls=%fused_computation.12.clone.1 | convolution fusion | flops 1080029184 | bytes 2375684 | tf_op jit(solution)/shard_map/while/body/eval_jaxpr/dot_general | solution.py:19
  95.3 3.4 %exponential_reduce_fusion.2 = f32[4096]{0:T(1024)S(1)} fusion(bf16[4096,256]{1,0:T(8,128)(2,1)} %get-tuple-element.1017, bf16[4,512,256]{2,1,0:T(8,128)(2,1)S(1)} %get-tuple-element.1016, s32[]{:T(128)} %get-tuple-element.1008), kind=kOutput, calls=%fused_computation.12.clone.1 | convolution fusion | flops 1080029184 | bytes 2375684 | tf_op jit(solution)/shard_map/while/body/eval_jaxpr/dot_general | solution.py:19
  98.7 9.2 %all-gather = f32[32768]{0:T(1024)S(1)} all-gather(f32[4096]{0:T(1024)S(1)} %get-tuple-element.457), channel_id=2, replica_groups=mesh['pts'=8,'lst'=4] {'pts'}, dimensions={0}, use_global_device_ids=true | all-gather | bytes 147456 | tf_op jit(solution)/shard_map/all_gather | solution.py:10
  108.0 15.0 %while.88 = (s32[]{:T(128)}, f32[4,512]{1,0:T(4,128)S(1)}, bf16[4,512,256]{2,1,0:T(8,128)(2,1)S(1)}, bf16[4096,256]{1,0:T(8,128)(2,1)}, f32[4096]{0:T(1024)S(1)}, /*index=5*/s32[]{:T(128)}, s32[]{:T(128)}) while((s32[]{:T(128)}, f32[4,512]{1,0:T(4,128)S(1)}, bf16[4,512,256]{2,1,0:T(8,128)(2,1)S(1)}, bf16[4096,256]{1,0:T(8,128)(2,1)}, ...), condition=%wide.region_8.9_spmd, body=%wide.region_6.8_spmd.sunk | while | flops 1082129920 | bytes 2381909 | solution.py:77
  108.0 3.7 %multiply_reduce_fusion.12 = f32[512]{0:T(512)S(1)} fusion(bf16[4096,256]{1,0:T(8,128)(2,1)} %get-tuple-element.1037, f32[4096]{0:T(1024)S(1)} %get-tuple-element.1038, bf16[4,512,256]{2,1,0:T(8,128)(2,1)S(1)} %get-tuple-element.1036, s32[]{:T(128)} %get-tuple-element.1027), kind=kOutput, calls=%fused_computation.clone.1 | convolution fusion | flops 1082129920 | bytes 2377732 | tf_op jit(solution)/shard_map/while/body/eval_jaxpr/dot_general | solution.py:19
  111.8 3.7 %multiply_reduce_fusion.12 = f32[512]{0:T(512)S(1)} fusion(bf16[4096,256]{1,0:T(8,128)(2,1)} %get-tuple-element.1037, f32[4096]{0:T(1024)S(1)} %get-tuple-element.1038, bf16[4,512,256]{2,1,0:T(8,128)(2,1)S(1)} %get-tuple-element.1036, s32[]{:T(128)} %get-tuple-element.1027), kind=kOutput, calls=%fused_computation.clone.1 | convolution fusion | flops 1082129920 | bytes 2377732 | tf_op jit(solution)/shard_map/while/body/eval_jaxpr/dot_general | solution.py:19
  115.5 3.7 %multiply_reduce_fusion.12 = f32[512]{0:T(512)S(1)} fusion(bf16[4096,256]{1,0:T(8,128)(2,1)} %get-tuple-element.1037, f32[4096]{0:T(1024)S(1)} %get-tuple-element.1038, bf16[4,512,256]{2,1,0:T(8,128)(2,1)S(1)} %get-tuple-element.1036, s32[]{:T(128)} %get-tuple-element.1027), kind=kOutput, calls=%fused_computation.clone.1 | convolution fusion | flops 1082129920 | bytes 2377732 | tf_op jit(solution)/shard_map/while/body/eval_jaxpr/dot_general | solution.py:19
  119.3 3.7 %multiply_reduce_fusion.12 = f32[512]{0:T(512)S(1)} fusion(bf16[4096,256]{1,0:T(8,128)(2,1)} %get-tuple-element.1037, f32[4096]{0:T(1024)S(1)} %get-tuple-element.1038, bf16[4,512,256]{2,1,0:T(8,128)(2,1)S(1)} %get-tuple-element.1036, s32[]{:T(128)} %get-tuple-element.1027), kind=kOutput, calls=%fused_computation.clone.1 | convolution fusion | flops 1082129920 | bytes 2377732 | tf_op jit(solution)/shard_map/while/body/eval_jaxpr/dot_general | solution.py:19
  123.1 10.3 %psum.21 = f32[2048]{0:T(1024)S(1)} all-reduce(f32[2048]{0:T(1024)S(1)} %bitcast.102), channel_id=1, replica_groups=mesh['pts'=8,'lst'=4] {'lst'}, use_global_device_ids=true, to_apply=%region_9.10 | all-reduce | flops 2048 | bytes 16384 | tf_op jit(solution)/shard_map/psum | solution.py:78
  133.4 14.9 %while.92 = (s32[]{:T(128)}, f32[4096]{0:T(1024)S(1)}, bf16[4,512,256]{2,1,0:T(8,128)(2,1)S(1)}, bf16[4096,256]{1,0:T(8,128)(2,1)}, f32[4,512]{1,0:T(4,128)S(1)}, /*index=5*/s32[]{:T(128)}, s32[]{:T(128)}) while((s32[]{:T(128)}, f32[4096]{0:T(1024)S(1)}, bf16[4,512,256]{2,1,0:T(8,128)(2,1)S(1)}, bf16[4096,256]{1,0:T(8,128)(2,1)}, ...), condition=%wide.region_12.13_spmd.clone, body=%wide.region_10.12_spmd.clone.sunk | while | flops 1082134528 | bytes 2431071 | solution.py:66
  133.4 3.7 %multiply_reduce_fusion.15 = f32[4096]{0:T(1024)S(1)} fusion(bf16[4096,256]{1,0:T(8,128)(2,1)} %get-tuple-element.1058, f32[512]{0:T(512)S(1)} %bitcast.97, bf16[4,512,256]{2,1,0:T(8,128)(2,1)S(1)} %get-tuple-element.1057, s32[]{:T(128)} %get-tuple-element.1048), kind=kOutput, calls=%fused_computation.17.clone.1 | convolution fusion | flops 1082126336 | bytes 2377732 | tf_op jit(solution)/shard_map/while/body/eval_jaxpr/dot_general | solution.py:19
  137.1 3.7 %multiply_reduce_fusion.15 = f32[4096]{0:T(1024)S(1)} fusion(bf16[4096,256]{1,0:T(8,128)(2,1)} %get-tuple-element.1058, f32[512]{0:T(512)S(1)} %bitcast.97, bf16[4,512,256]{2,1,0:T(8,128)(2,1)S(1)} %get-tuple-element.1057, s32[]{:T(128)} %get-tuple-element.1048), kind=kOutput, calls=%fused_computation.17.clone.1 | convolution fusion | flops 1082126336 | bytes 2377732 | tf_op jit(solution)/shard_map/while/body/eval_jaxpr/dot_general | solution.py:19
  140.8 3.7 %multiply_reduce_fusion.15 = f32[4096]{0:T(1024)S(1)} fusion(bf16[4096,256]{1,0:T(8,128)(2,1)} %get-tuple-element.1058, f32[512]{0:T(512)S(1)} %bitcast.97, bf16[4,512,256]{2,1,0:T(8,128)(2,1)S(1)} %get-tuple-element.1057, s32[]{:T(128)} %get-tuple-element.1048), kind=kOutput, calls=%fused_computation.17.clone.1 | convolution fusion | flops 1082126336 | bytes 2377732 | tf_op jit(solution)/shard_map/while/body/eval_jaxpr/dot_general | solution.py:19
  144.6 3.7 %multiply_reduce_fusion.15 = f32[4096]{0:T(1024)S(1)} fusion(bf16[4096,256]{1,0:T(8,128)(2,1)} %get-tuple-element.1058, f32[512]{0:T(512)S(1)} %bitcast.97, bf16[4,512,256]{2,1,0:T(8,128)(2,1)S(1)} %get-tuple-element.1057, s32[]{:T(128)} %get-tuple-element.1048), kind=kOutput, calls=%fused_computation.17.clone.1 | convolution fusion | flops 1082126336 | bytes 2377732 | tf_op jit(solution)/shard_map/while/body/eval_jaxpr/dot_general | solution.py:19
  148.3 9.2 %all-gather.1 = f32[32768]{0:T(1024)S(1)} all-gather(f32[4096]{0:T(1024)S(1)} %get-tuple-element.459), channel_id=3, replica_groups=mesh['pts'=8,'lst'=4] {'pts'}, dimensions={0}, use_global_device_ids=true | all-gather | bytes 147456 | tf_op jit(solution)/shard_map/all_gather | solution.py:10
  157.5 15.0 %while.89 = (s32[]{:T(128)}, f32[4,512]{1,0:T(4,128)S(1)}, bf16[4,512,256]{2,1,0:T(8,128)(2,1)S(1)}, bf16[4096,256]{1,0:T(8,128)(2,1)}, f32[4096]{0:T(1024)S(1)}, /*index=5*/s32[]{:T(128)}, s32[]{:T(128)}) while((s32[]{:T(128)}, f32[4,512]{1,0:T(4,128)S(1)}, bf16[4,512,256]{2,1,0:T(8,128)(2,1)S(1)}, bf16[4096,256]{1,0:T(8,128)(2,1)}, ...), condition=%wide.region_16.17_spmd, body=%wide.region_14.16_spmd.sunk | while | flops 1082129920 | bytes 2381909 | solution.py:77
  157.6 3.7 %multiply_reduce_fusion.13 = f32[512]{0:T(512)S(1)} fusion(bf16[4096,256]{1,0:T(8,128)(2,1)} %get-tuple-element.1079, f32[4096]{0:T(1024)S(1)} %get-tuple-element.1080, bf16[4,512,256]{2,1,0:T(8,128)(2,1)S(1)} %get-tuple-element.1078, s32[]{:T(128)} %get-tuple-element.1069), kind=kOutput, calls=%fused_computation.4.clone.1 | convolution fusion | flops 1082129920 | bytes 2377732 | tf_op jit(solution)/shard_map/while/body/eval_jaxpr/dot_general | solution.py:19
  161.3 3.7 %multiply_reduce_fusion.13 = f32[512]{0:T(512)S(1)} fusion(bf16[4096,256]{1,0:T(8,128)(2,1)} %get-tuple-element.1079, f32[4096]{0:T(1024)S(1)} %get-tuple-element.1080, bf16[4,512,256]{2,1,0:T(8,128)(2,1)S(1)} %get-tuple-element.1078, s32[]{:T(128)} %get-tuple-element.1069), kind=kOutput, calls=%fused_computation.4.clone.1 | convolution fusion | flops 1082129920 | bytes 2377732 | tf_op jit(solution)/shard_map/while/body/eval_jaxpr/dot_general | solution.py:19
  165.1 3.7 %multiply_reduce_fusion.13 = f32[512]{0:T(512)S(1)} fusion(bf16[4096,256]{1,0:T(8,128)(2,1)} %get-tuple-element.1079, f32[4096]{0:T(1024)S(1)} %get-tuple-element.1080, bf16[4,512,256]{2,1,0:T(8,128)(2,1)S(1)} %get-tuple-element.1078, s32[]{:T(128)} %get-tuple-element.1069), kind=kOutput, calls=%fused_computation.4.clone.1 | convolution fusion | flops 1082129920 | bytes 2377732 | tf_op jit(solution)/shard_map/while/body/eval_jaxpr/dot_general | solution.py:19
  168.8 3.7 %multiply_reduce_fusion.13 = f32[512]{0:T(512)S(1)} fusion(bf16[4096,256]{1,0:T(8,128)(2,1)} %get-tuple-element.1079, f32[4096]{0:T(1024)S(1)} %get-tuple-element.1080, bf16[4,512,256]{2,1,0:T(8,128)(2,1)S(1)} %get-tuple-element.1078, s32[]{:T(128)} %get-tuple-element.1069), kind=kOutput, calls=%fused_computation.4.clone.1 | convolution fusion | flops 1082129920 | bytes 2377732 | tf_op jit(solution)/shard_map/while/body/eval_jaxpr/dot_general | solution.py:19
  172.6 8.9 %psum.22 = f32[2048]{0:T(1024)S(1)} all-reduce(f32[2048]{0:T(1024)S(1)} %bitcast.103), channel_id=1, replica_groups=mesh['pts'=8,'lst'=4] {'lst'}, use_global_device_ids=true, to_apply=%region_17.18 | all-reduce | flops 2048 | bytes 16384 | tf_op jit(solution)/shard_map/psum | solution.py:78
  181.6 14.8 %while.93 = (s32[]{:T(128)}, f32[4096]{0:T(1024)S(1)}, bf16[4,512,256]{2,1,0:T(8,128)(2,1)S(1)}, bf16[4096,256]{1,0:T(8,128)(2,1)}, f32[4,512]{1,0:T(4,128)S(1)}, /*index=5*/s32[]{:T(128)}, s32[]{:T(128)}) while((s32[]{:T(128)}, f32[4096]{0:T(1024)S(1)}, bf16[4,512,256]{2,1,0:T(8,128)(2,1)S(1)}, bf16[4096,256]{1,0:T(8,128)(2,1)}, ...), condition=%wide.region_20.21_spmd.clone, body=%wide.region_18.20_spmd.clone.sunk | while | flops 1082134528 | bytes 2431071 | solution.py:66
  181.6 3.7 %multiply_reduce_fusion.16 = f32[4096]{0:T(1024)S(1)} fusion(bf16[4096,256]{1,0:T(8,128)(2,1)} %get-tuple-element.1100, f32[512]{0:T(512)S(1)} %bitcast.98, bf16[4,512,256]{2,1,0:T(8,128)(2,1)S(1)} %get-tuple-element.1099, s32[]{:T(128)} %get-tuple-element.1090), kind=kOutput, calls=%fused_computation.23.clone.1 | convolution fusion | flops 1082126336 | bytes 2377732 | tf_op jit(solution)/shard_map/while/body/eval_jaxpr/dot_general | solution.py:19
  185.3 3.7 %multiply_reduce_fusion.16 = f32[4096]{0:T(1024)S(1)} fusion(bf16[4096,256]{1,0:T(8,128)(2,1)} %get-tuple-element.1100, f32[512]{0:T(512)S(1)} %bitcast.98, bf16[4,512,256]{2,1,0:T(8,128)(2,1)S(1)} %get-tuple-element.1099, s32[]{:T(128)} %get-tuple-element.1090), kind=kOutput, calls=%fused_computation.23.clone.1 | convolution fusion | flops 1082126336 | bytes 2377732 | tf_op jit(solution)/shard_map/while/body/eval_jaxpr/dot_general | solution.py:19
  189.0 3.7 %multiply_reduce_fusion.16 = f32[4096]{0:T(1024)S(1)} fusion(bf16[4096,256]{1,0:T(8,128)(2,1)} %get-tuple-element.1100, f32[512]{0:T(512)S(1)} %bitcast.98, bf16[4,512,256]{2,1,0:T(8,128)(2,1)S(1)} %get-tuple-element.1099, s32[]{:T(128)} %get-tuple-element.1090), kind=kOutput, calls=%fused_computation.23.clone.1 | convolution fusion | flops 1082126336 | bytes 2377732 | tf_op jit(solution)/shard_map/while/body/eval_jaxpr/dot_general | solution.py:19
  192.7 3.7 %multiply_reduce_fusion.16 = f32[4096]{0:T(1024)S(1)} fusion(bf16[4096,256]{1,0:T(8,128)(2,1)} %get-tuple-element.1100, f32[512]{0:T(512)S(1)} %bitcast.98, bf16[4,512,256]{2,1,0:T(8,128)(2,1)S(1)} %get-tuple-element.1099, s32[]{:T(128)} %get-tuple-element.1090), kind=kOutput, calls=%fused_computation.23.clone.1 | convolution fusion | flops 1082126336 | bytes 2377732 | tf_op jit(solution)/shard_map/while/body/eval_jaxpr/dot_general | solution.py:19
  196.4 8.3 %all-gather.2 = f32[32768]{0:T(1024)S(1)} all-gather(f32[4096]{0:T(1024)S(1)} %get-tuple-element.461), channel_id=4, replica_groups=mesh['pts'=8,'lst'=4] {'pts'}, dimensions={0}, use_global_device_ids=true | all-gather | bytes 147456 | tf_op jit(solution)/shard_map/all_gather | solution.py:10
  204.8 15.1 %while.90 = (s32[]{:T(128)}, f32[4,512]{1,0:T(4,128)S(1)}, bf16[4,512,256]{2,1,0:T(8,128)(2,1)S(1)}, bf16[4096,256]{1,0:T(8,128)(2,1)}, f32[4096]{0:T(1024)S(1)}, /*index=5*/s32[]{:T(128)}, s32[]{:T(128)}) while((s32[]{:T(128)}, f32[4,512]{1,0:T(4,128)S(1)}, bf16[4,512,256]{2,1,0:T(8,128)(2,1)S(1)}, bf16[4096,256]{1,0:T(8,128)(2,1)}, ...), condition=%wide.region_24.25_spmd, body=%wide.region_22.24_spmd.sunk | while | flops 1082129920 | bytes 2381909 | solution.py:77
  204.8 3.7 %multiply_reduce_fusion.14 = f32[512]{0:T(512)S(1)} fusion(bf16[4096,256]{1,0:T(8,128)(2,1)} %get-tuple-element.1121, f32[4096]{0:T(1024)S(1)} %get-tuple-element.1122, bf16[4,512,256]{2,1,0:T(8,128)(2,1)S(1)} %get-tuple-element.1120, s32[]{:T(128)} %get-tuple-element.1111), kind=kOutput, calls=%fused_computation.8.clone.1 | convolution fusion | flops 1082129920 | bytes 2377732 | tf_op jit(solution)/shard_map/while/body/eval_jaxpr/dot_general | solution.py:19
  208.6 3.7 %multiply_reduce_fusion.14 = f32[512]{0:T(512)S(1)} fusion(bf16[4096,256]{1,0:T(8,128)(2,1)} %get-tuple-element.1121, f32[4096]{0:T(1024)S(1)} %get-tuple-element.1122, bf16[4,512,256]{2,1,0:T(8,128)(2,1)S(1)} %get-tuple-element.1120, s32[]{:T(128)} %get-tuple-element.1111), kind=kOutput, calls=%fused_computation.8.clone.1 | convolution fusion | flops 1082129920 | bytes 2377732 | tf_op jit(solution)/shard_map/while/body/eval_jaxpr/dot_general | solution.py:19
  212.3 3.7 %multiply_reduce_fusion.14 = f32[512]{0:T(512)S(1)} fusion(bf16[4096,256]{1,0:T(8,128)(2,1)} %get-tuple-element.1121, f32[4096]{0:T(1024)S(1)} %get-tuple-element.1122, bf16[4,512,256]{2,1,0:T(8,128)(2,1)S(1)} %get-tuple-element.1120, s32[]{:T(128)} %get-tuple-element.1111), kind=kOutput, calls=%fused_computation.8.clone.1 | convolution fusion | flops 1082129920 | bytes 2377732 | tf_op jit(solution)/shard_map/while/body/eval_jaxpr/dot_general | solution.py:19
  216.1 3.7 %multiply_reduce_fusion.14 = f32[512]{0:T(512)S(1)} fusion(bf16[4096,256]{1,0:T(8,128)(2,1)} %get-tuple-element.1121, f32[4096]{0:T(1024)S(1)} %get-tuple-element.1122, bf16[4,512,256]{2,1,0:T(8,128)(2,1)S(1)} %get-tuple-element.1120, s32[]{:T(128)} %get-tuple-element.1111), kind=kOutput, calls=%fused_computation.8.clone.1 | convolution fusion | flops 1082129920 | bytes 2377732 | tf_op jit(solution)/shard_map/while/body/eval_jaxpr/dot_general | solution.py:19
  219.9 10.3 %psum.23 = f32[2048]{0:T(1024)S(1)} all-reduce(f32[2048]{0:T(1024)S(1)} %bitcast.104), channel_id=1, replica_groups=mesh['pts'=8,'lst'=4] {'lst'}, use_global_device_ids=true, to_apply=%region_25.26 | all-reduce | flops 2048 | bytes 16384 | tf_op jit(solution)/shard_map/psum | solution.py:78
  230.2 0.6 fusion.28
  230.8 31.3 %while.94 = (s32[]{:T(128)}, f32[4096,256]{1,0:T(8,128)}, f32[4,512]{1,0:T(4,128)S(1)}, bf16[4,512,256]{2,1,0:T(8,128)(2,1)S(1)}, bf16[4096,256]{1,0:T(8,128)(2,1)}, /*index=5*/f32[4096]{0:T(1024)S(1)}, s32[]{:T(128)}, s32[]{:T(128)}) while((s32[]{:T(128)}, f32[4096,256]{1,0:T(8,128)}, f32[4,512]{1,0:T(4,128)S(1)}, ...), condition=%wide.region_27.28_spmd.clone, body=%wide.region_26.27_spmd.clone.sunk | while | flops 2160066560 | bytes 11033699 | solution.py:87
  230.8 6.9 %convolution_add_fusion.2 = f32[4096,256]{1,0:T(8,128)} fusion(f32[4096,256]{1,0:T(8,128)} %get-tuple-element.1134, pred[]{:T(512)S(6)} %compare.15, bf16[4096,256]{1,0:T(8,128)(2,1)} %get-tuple-element.1145, f32[4096]{0:T(1024)S(1)} %get-tuple-element.1146, f32[512]{0:T(512)S(1)} %bitcast.93, bf16[4,512,256]{2,1,0:T(8,128)(2,1)S(1)} %get-tuple-element.1144, ...), kind=kOutput, calls=%fused_computation.30.clone.1 | convolution fusion | flops 2160066560 | bytes 11029505 | tf_op jit(solution)/shard_map/while/body/eval_jaxpr/dot_general | solution.py:27
  237.7 8.1 %convolution_add_fusion.2 = f32[4096,256]{1,0:T(8,128)} fusion(f32[4096,256]{1,0:T(8,128)} %get-tuple-element.1134, pred[]{:T(512)S(6)} %compare.15, bf16[4096,256]{1,0:T(8,128)(2,1)} %get-tuple-element.1145, f32[4096]{0:T(1024)S(1)} %get-tuple-element.1146, f32[512]{0:T(512)S(1)} %bitcast.93, bf16[4,512,256]{2,1,0:T(8,128)(2,1)S(1)} %get-tuple-element.1144, ...), kind=kOutput, calls=%fused_computation.30.clone.1 | convolution fusion | flops 2160066560 | bytes 11029505 | tf_op jit(solution)/shard_map/while/body/eval_jaxpr/dot_general | solution.py:27
  245.8 8.1 %convolution_add_fusion.2 = f32[4096,256]{1,0:T(8,128)} fusion(f32[4096,256]{1,0:T(8,128)} %get-tuple-element.1134, pred[]{:T(512)S(6)} %compare.15, bf16[4096,256]{1,0:T(8,128)(2,1)} %get-tuple-element.1145, f32[4096]{0:T(1024)S(1)} %get-tuple-element.1146, f32[512]{0:T(512)S(1)} %bitcast.93, bf16[4,512,256]{2,1,0:T(8,128)(2,1)S(1)} %get-tuple-element.1144, ...), kind=kOutput, calls=%fused_computation.30.clone.1 | convolution fusion | flops 2160066560 | bytes 11029505 | tf_op jit(solution)/shard_map/while/body/eval_jaxpr/dot_general | solution.py:27
  253.9 8.1 %convolution_add_fusion.2 = f32[4096,256]{1,0:T(8,128)} fusion(f32[4096,256]{1,0:T(8,128)} %get-tuple-element.1134, pred[]{:T(512)S(6)} %compare.15, bf16[4096,256]{1,0:T(8,128)(2,1)} %get-tuple-element.1145, f32[4096]{0:T(1024)S(1)} %get-tuple-element.1146, f32[512]{0:T(512)S(1)} %bitcast.93, bf16[4,512,256]{2,1,0:T(8,128)(2,1)S(1)} %get-tuple-element.1144, ...), kind=kOutput, calls=%fused_computation.30.clone.1 | convolution fusion | flops 2160066560 | bytes 11029505 | tf_op jit(solution)/shard_map/while/body/eval_jaxpr/dot_general | solution.py:27
  262.1 0.0 reduce-scatter.2.cloned.1.call-update
  262.1 48.6 %reduce-scatter.2.cloned.1.call-done = f32[512,256]{1,0:T(8,128)} async-done(((f32[4096,256]{1,0:T(8,128)}), f32[512,256]{1,0:T(8,128)}) %reduce-scatter.2.cloned.1.call-update) | async-done | bytes 524304 | tf_op jit(solution)/shard_map/reduce_scatter | solution.py:90
  310.7 1.2 multiply_reduce_fusion.5
  311.9 2.0 broadcast_multiply_fusion
  (63 shorter events, 1.0 us)
Async XLA Ops:
  7.2 47.2 %copy-start = (bf16[4096,256]{1,0:T(8,128)(2,1)S(1)}, bf16[4096,256]{1,0:T(8,128)(2,1)}, u32[]{:S(2)}) copy-start(bf16[4096,256]{1,0:T(8,128)(2,1)} %param.19) | copy-start | bytes 6291460
  7.2 43.1 %all-to-all-start = ((bf16[4,512,256]{2,1,0:T(8,128)(2,1)}), bf16[4,512,256]{2,1,0:T(8,128)(2,1)S(1)}, u32[]{:S(2)}, u32[]{:S(2)}) async-start(bf16[4,512,256]{2,1,0:T(8,128)(2,1)} %bitcast.90), calls=%async_computation | async-start | bytes 2097152 | tf_op jit(solution)/shard_map/all_to_all | solution.py:42
  13.7 69.8 %all-gather.5.cloned.1.call-start = ((), (), s32[]{:S(2)}) async-start(), calls=%async_computation.2 | async-start | bytes 1310720 | tf_op jit(solution)/shard_map/all_gather | solution.py:48
  54.2 256.4 %reduce-scatter.2.cloned.1.call-start = ((), (), s32[]{:S(2)}) async-start(), calls=%async_computation.3 | async-start | bytes 4718592 | tf_op jit(solution)/shard_map/reduce_scatter | solution.py:90
Sparse Core Ops, SparseCore 0:
  54.3 29.1 all-gather.4
  262.2 48.4 reduce-scatter.1
